TPU v7x, 256 devices: a whole 4x4x8 slice. The times are simulated.
256 devices in a mesh: gx: 8 (over z), gy: 4 (over x), gz: 8 (over y, core).
Axes of the slice: x: 4, y: 4, z: 8, core: 2. Of those that a mesh axis runs over, the one named last changes fastest.
Arguments:
- field: float32 [1024, 1024, 512], P('gz', 'gx', 'gy'), may hold values from -6 to 6
- peaks: float32 [4], replicated, may hold values from -1.5 to 1.5
- tint: float32 [3], replicated, may hold values from -2 to 2
- light: float32 [3], replicated, may hold values from -1 to 1
Outputs:
- image: float32 [4, 1024, 512], P(None, ('gx', 'gz'), 'gy')
All inputs are finite; a program needn't handle non-finite values.
Results may differ from a plain program's by a relative error of at most 0.0003.
Values sent between devices are 32-bit elements; how exact they have to be, the bound alone decides.
A program may use at most 256 MiB of HBM per device.

v0:
```python
import functools
import math

import jax
import jax.numpy as jnp
from jax import lax
from jax.experimental import pallas as pl
from jax.experimental.pallas import tpu as pltpu
from jax.sharding import PartitionSpec as P

extinction = 1.5
LOG2E = math.log2(math.e)
MESH = pl.DeviceIdType.MESH
ROWS = 16
GROUP = 32
UNROLL = 32


def kernel(
    nx, ny, nz, depth, field, peaks, tint, light, out,
    cells, eighth, border, to_right, to_left, from_left, from_right, piece, pieces,
    load_sem, x_send, x_recv, z_send, z_recv, y_send, y_recv, p_send, p_recv,
):
    zs, xs, lanes = field.shape
    groups = zs // GROUP
    blocks = xs // ROWS
    mx, my, mz = lax.axis_index("gx"), lax.axis_index("gy"), lax.axis_index("gz")
    left_x, right_x = lax.rem(mx + nx - 1, nx), lax.rem(mx + 1, nx)
    left_y, right_y = lax.rem(my + ny - 1, ny), lax.rem(my + 1, ny)
    left_z, right_z = lax.rem(mz + nz - 1, nz), lax.rem(mz + 1, nz)

    def block_of(step):
        return lax.rem(mz + 1 + step, nz)

    def rows_of(step):
        return pl.multiple_of(block_of(step) * ROWS, ROWS)

    def load(step):
        return pltpu.make_async_copy(
            field.at[:, pl.ds(rows_of(step), ROWS), :],
            cells.at[2 : zs + 2, pl.ds(rows_of(step) + 8, ROWS), :],
            load_sem.at[step],
        )

    for step in range(blocks):
        load(step).start()

    barrier = pltpu.get_barrier_semaphore()
    greeted = 0
    for name, who in (("gx", left_x), ("gx", right_x), ("gy", left_y), ("gy", right_y)):
        pl.semaphore_signal(barrier, inc=1, device_id={name: who}, device_id_type=MESH)
        greeted += 1
    for k in range(1, nz):
        pl.semaphore_signal(
            barrier, inc=1, device_id={"gz": lax.rem(mz + k, nz)}, device_id_type=MESH
        )
        greeted += 1

    lane = lax.broadcasted_iota(jnp.int32, (ROWS, lanes), 1)
    lane_group = lane >> 2
    lane_column = lane & 3
    first_pair = lane_column < 2

    def pack(step):
        rows = rows_of(step)

        packed = [jnp.zeros((ROWS, lanes), jnp.float32)] * groups
        for z in range(GROUP):
            here = lane_group == z
            for g in range(groups):
                v = cells[2 + g * GROUP + z, pl.ds(rows + 8, ROWS), :]
                eighth[2 + g * GROUP + z, pl.ds(rows + 8, ROWS), :] = 0.125 * v
                packed[g] = jnp.where(here, pltpu.roll(v, (4 * z + 2) % lanes, 1), packed[g])
        for g in range(groups):
            border[g, pl.ds(rows, ROWS), :] = packed[g]
        for g in range(0, groups, 2):
            even, odd = packed[g], packed[g + 1]
            to_right[step, g // 2] = jnp.where(first_pair, even, pltpu.roll(odd, 2, 1))
            to_left[step, g // 2] = jnp.where(first_pair, pltpu.roll(odd, lanes - 2, 1), even)

    def y_copies(step):
        right = pltpu.make_async_remote_copy(
            to_right.at[step], from_left.at[step], y_send.at[0, step], y_recv.at[0, step],
            device_id={"gy": right_y}, device_id_type=MESH,
        )
        left = pltpu.make_async_remote_copy(
            to_left.at[step], from_right.at[step], y_send.at[1, step], y_recv.at[1, step],
            device_id={"gy": left_y}, device_id_type=MESH,
        )
        return right, left

    inner = pl.ds(8, xs)
    halos = [
        pltpu.make_async_remote_copy(
            field.at[zs - 2 : zs], cells.at[0:2, inner, :], z_send.at[0], z_recv.at[0],
            device_id={"gz": right_z}, device_id_type=MESH,
        ),
        pltpu.make_async_remote_copy(
            field.at[0:2], cells.at[zs + 2 : zs + 4, inner, :], z_send.at[1], z_recv.at[1],
            device_id={"gz": left_z}, device_id_type=MESH,
        ),
        pltpu.make_async_remote_copy(
            field.at[:, xs - 2 : xs, :], cells.at[2 : zs + 2, 6:8, :], x_send.at[0], x_recv.at[0],
            device_id={"gx": right_x}, device_id_type=MESH,
        ),
        pltpu.make_async_remote_copy(
            field.at[:, 0:2, :], cells.at[2 : zs + 2, xs + 8 : xs + 10, :], x_send.at[1],
            x_recv.at[1], device_id={"gx": left_x}, device_id_type=MESH,
        ),
    ]

    load(0).wait()
    pack(0)
    pl.semaphore_wait(barrier, greeted)
    for copy in halos:
        copy.start()
    for copy in y_copies(0):
        copy.start()

    @pl.loop(1, blocks)
    def _(step):
        load(step).wait()
        pack(step)
        for copy in y_copies(step):
            copy.start()

    def correction(step):
        rows = rows_of(step)
        for g in range(0, groups, 2):
            left, right = from_left[step, g // 2], from_right[step, g // 2]
            for odd in range(2):
                if odd:
                    outer = jnp.where(
                        first_pair, pltpu.roll(left, lanes - 2, 1), pltpu.roll(right, 2, 1)
                    )
                else:
                    outer = jnp.where(first_pair, left, right)
                diff = outer - border[g + odd, pl.ds(rows, ROWS), :]
                p2, p1 = pltpu.roll(diff, lanes - 2, 1), pltpu.roll(diff, lanes - 1, 1)
                m2, m1 = pltpu.roll(diff, 2, 1), pltpu.roll(diff, 1, 1)
                far = 0.125 * jnp.where(first_pair, -p2, m2)
                near = jnp.where(lane_column == 1, p1, jnp.where(lane_column == 2, -m1, 0.0))
                border[g + odd, pl.ds(rows, ROWS), :] = near + far

    unit = extinction / depth * LOG2E
    first = peaks[0]
    slopes = [4.0 * LOG2E * (peaks[i] - first) for i in range(1, peaks.shape[0])]
    offsets = [
        math.log2(unit) - 2.0 * LOG2E * (peaks[i] * peaks[i] - first * first)
        for i in range(1, peaks.shape[0])
    ]
    tints = [0.5 * tint[c] for c in range(3)]
    lights = [0.7 * light[c] for c in range(3)]
    edge = (lane < 2) | (lane >= lanes - 2)

    def march(step):
        rows = rows_of(step)
        base = rows + 8
        mid = pl.ds(base, ROWS)

        def one_group(g, carry):
            fix_all = border[g, pl.ds(rows, ROWS), :]

            def some(i, carry):
                total, trans, s0, s1, s2, s3 = carry
                for j in range(UNROLL):
                    zl = i * UNROLL + j
                    z = g * GROUP + zl + 2
                    f, f8 = cells[z, mid, :], eighth[z, mid, :]
                    gz = (cells[z + 1, mid, :] - cells[z - 1, mid, :]) - (
                        eighth[z + 2, mid, :] - eighth[z - 2, mid, :]
                    )
                    gx = (
                        cells[z, pl.ds(base + 1, ROWS), :] - cells[z, pl.ds(base - 1, ROWS), :]
                    ) - (eighth[z, pl.ds(base + 2, ROWS), :] - eighth[z, pl.ds(base - 2, ROWS), :])
                    gy = (pltpu.roll(f, lanes - 1, 1) - pltpu.roll(f, 1, 1)) - (
                        pltpu.roll(f8, lanes - 2, 1) - pltpu.roll(f8, 2, 1)
                    )
                    fix = pltpu.roll(fix_all, (2 * lanes - 2 - 4 * zl) % lanes, 1)
                    gy = jnp.where(edge, gy + fix, gy)
                    inverse = lax.rsqrt((gx * gx + gy * gy) + (gz * gz + 2.25))
                    lit = jnp.abs(gx * lights[0] + gy * lights[1] + gz * lights[2])
                    bumps = unit
                    for k in range(len(slopes)):
                        bumps = bumps + jnp.exp2(f * slopes[k] + offsets[k])
                    away = f - first
                    total = total - jnp.exp2(away * away * (-2.0 * LOG2E)) * bumps
                    after = jnp.exp2(total)
                    shaded = (trans - after) * (0.3 + lit * inverse)
                    trans = after
                    s0 = s0 + shaded
                    s1 = s1 + shaded * jnp.tanh(f * tints[0])
                    s2 = s2 + shaded * jnp.tanh(f * tints[1])
                    s3 = s3 + shaded * jnp.tanh(f * tints[2])
                return total, trans, s0, s1, s2, s3

            if UNROLL == GROUP:
                return some(0, carry)
            return lax.fori_loop(0, GROUP // UNROLL, some, carry)

        zero = jnp.zeros((ROWS, lanes), jnp.float32)
        start = (zero, zero + 1.0, zero, zero, zero, zero)
        total, _, s0, s1, s2, s3 = lax.fori_loop(0, groups, one_group, start)
        return 0.5 * (s0 + s1), 0.5 * (s0 + s2), 0.5 * (s0 + s3), total

    def p_copy(step):
        return pltpu.make_async_remote_copy(
            piece.at[step], pieces.at[mz], p_send.at[step], p_recv.at[mz],
            device_id={"gz": block_of(step)}, device_id_type=MESH,
        )

    for copy in halos:
        copy.wait_recv()
    for z in (0, 1, zs + 2, zs + 3):
        eighth[z, inner, :] = 0.125 * cells[z, inner, :]

    @pl.loop(0, zs // 8)
    def _(i):
        for rows in (pl.ds(6, 2), pl.ds(xs + 8, 2)):
            eighth[pl.ds(i * 8 + 2, 8), rows, :] = 0.125 * cells[pl.ds(i * 8 + 2, 8), rows, :]

    @pl.loop(0, blocks)
    def _(step):
        for copy in y_copies(step):
            copy.wait_recv()
        correction(step)
        results = march(step)

        @pl.when(step < blocks - 1)
        def _():
            for c in range(4):
                piece[step, c] = results[c]
            p_copy(step).start()

        @pl.when(step == blocks - 1)
        def _():
            for c in range(4):
                pieces[mz, c] = results[c]

    for k in range(1, nz):
        source = lax.rem(mz + k, nz)
        pltpu.make_async_remote_copy(
            piece.at[0], pieces.at[source], p_send.at[0], p_recv.at[source],
            device_id={"gz": source}, device_id_type=MESH,
        ).wait_recv()

    before = None
    for k in range(nz):
        if k == 0:
            image = [pieces[0, c] for c in range(3)]
            optical = pieces[0, 3]
        else:
            before = jnp.exp2(optical)
            image = [image[c] + before * pieces[k, c] for c in range(3)]
            optical = optical + pieces[k, 3]
    for c in range(3):
        out[c] = image[c]
    out[3] = 1.0 - jnp.exp2(optical)

    for copy in halos:
        copy.wait_send()
    for step in range(blocks):
        for copy in y_copies(step):
            copy.wait_send()
    for step in range(blocks - 1):
        p_copy(step).wait_send()


def render(sizes, field, peaks, tint, light):
    nx, ny, nz = sizes
    zs, xs, lanes = field.shape
    groups, blocks = zs // GROUP, xs // ROWS
    f32 = jnp.float32
    packed = pltpu.VMEM((blocks, groups // 2, ROWS, lanes), f32)
    dma = pltpu.SemaphoreType.DMA
    smem = pl.BlockSpec(memory_space=pltpu.SMEM)
    return pl.pallas_call(
        functools.partial(kernel, nx, ny, nz, zs * nz),
        out_shape=jax.ShapeDtypeStruct((4, ROWS, lanes), f32),
        in_specs=[pl.BlockSpec(memory_space=pl.ANY), smem, smem, smem],
        out_specs=pl.BlockSpec(memory_space=pltpu.VMEM),
        scratch_shapes=[
            pltpu.VMEM((zs + 4, xs + 16, lanes), f32),
            pltpu.VMEM((zs + 4, xs + 16, lanes), f32),
            pltpu.VMEM((groups, xs, lanes), f32),
            packed, packed, packed, packed,
            pltpu.VMEM((blocks, 4, ROWS, lanes), f32),
            pltpu.VMEM((nz, 4, ROWS, lanes), f32),
            dma((blocks,)), dma((2,)), dma((2,)), dma((2,)), dma((2,)),
            dma((2, blocks)), dma((2, blocks)), dma((blocks,)), dma((nz,)),
        ],
        compiler_params=pltpu.CompilerParams(collective_id=0, has_side_effects=True),
    )(field, peaks, tint, light)


def solution(mesh):
    sizes = (mesh.shape["gx"], mesh.shape["gy"], mesh.shape["gz"])
    in_specs = (P("gz", "gx", "gy"), P(), P(), P())
    out_specs = P(None, ("gx", "gz"), "gy")
    return jax.shard_map(
        functools.partial(render, sizes),
        mesh=mesh, in_specs=in_specs, out_specs=out_specs, check_vma=False,
    )
```

profile of v0, /device:TPU:1, one launch (start us, length us, event | category | flops | bytes accessed | tf_op | source)
XLA Modules:
  0.0 37.1 jit_solution(4319840096770183138)
XLA Ops:
  0.0 35.8 %shard_map.46 = f32[4,16,128]{2,1,0:T(8,128)} custom-call(f32[128,128,128]{2,1,0:T(8,128)} %field.1, f32[4]{0:T(128)} %peaks.1, f32[3]{0:T(128)} %tint.1, f32[3]{0:T(128)} %light.1), custom_call_target="tpu_custom_call" | custom-call | tf_op jit(solution)/shard_map/pallas_call | solution.py:277
  35.8 1.4 %copy.6 = f32[4,16,128]{2,1,0:T(8,128)} copy(f32[4,16,128]{2,1,0:T(8,128)} %shard_map.46) | data formatting | bytes 65536
where the time goes:
time: 37.3 us; the launch traced here: 37.1 us
  Pallas kernels  35.8 us (96%)
  local copies, waits for them, and re-layouts  1.38 us (4%)
    pallas_call x1, Pallas kernels, render(): pl.pallas_call(functools.partial(kernel, nx, ny, nz, zs * nz), out_shape=...  35.8 us
    unnamed x1, local copies, waits for them, and re-layouts  1.38 us

commit v1 on v0

--- a/solution.py
+++ b/solution.py
@@ -14,12 +14,13 @@
 ROWS = 16
 GROUP = 32
 UNROLL = 32
+SEND_X = 1
 
 
 def kernel(
     nx, ny, nz, depth, field, peaks, tint, light, out,
     cells, eighth, border, to_right, to_left, from_left, from_right, piece, pieces,
-    load_sem, x_send, x_recv, z_send, z_recv, y_send, y_recv, p_send, p_recv,
+    load_sem, x_send, x_recv, z_send, z_recv, y_send, y_recv, p_send, p_recv, entered,
 ):
     zs, xs, lanes = field.shape
     groups = zs // GROUP
@@ -29,8 +30,20 @@
     left_y, right_y = lax.rem(my + ny - 1, ny), lax.rem(my + 1, ny)
     left_z, right_z = lax.rem(mz + nz - 1, nz), lax.rem(mz + 1, nz)
 
+    bordering = 1 - (lax.rem(mz, nz - 1) + nz - 2) // (nz - 1)
+    parity = lax.rem(mz, 2)
+
     def block_of(step):
-        return lax.rem(mz + 1 + step, nz)
+        from_0, from_1, from_2 = ((step + k) // nz for k in (3, 2, 1))
+        inside = lax.rem(mz + step, nz - 2) + 1
+        border_one = bordering * inside + (1 - bordering) * parity * (nz - 1)
+        border_two = bordering * (nz - 1 - mz) + (1 - bordering) * (1 - parity) * (nz - 1)
+        return (
+            (1 - from_0) * inside
+            + (from_0 - from_1) * border_one
+            + (from_1 - from_2) * border_two
+            + from_2 * mz
+        )
 
     def rows_of(step):
         return pl.multiple_of(block_of(step) * ROWS, ROWS)
@@ -46,15 +59,23 @@
         load(step).start()
 
     barrier = pltpu.get_barrier_semaphore()
-    greeted = 0
-    for name, who in (("gx", left_x), ("gx", right_x), ("gy", left_y), ("gy", right_y)):
-        pl.semaphore_signal(barrier, inc=1, device_id={name: who}, device_id_type=MESH)
-        greeted += 1
+    above_first, at_last = (mx + nx - 1) // nx, (mx + 1) // nx
+
+    @pl.when(mx < nx - 1)
+    def _():
+        pl.semaphore_signal(barrier, inc=1, device_id={"gx": right_x}, device_id_type=MESH)
+
+    @pl.when(mx == 0)
+    def _():
+        pl.semaphore_signal(barrier, inc=1, device_id={"gx": left_x}, device_id_type=MESH)
+
+    for who in (left_y, right_y):
+        pl.semaphore_signal(barrier, inc=1, device_id={"gy": who}, device_id_type=MESH)
     for k in range(1, nz):
         pl.semaphore_signal(
             barrier, inc=1, device_id={"gz": lax.rem(mz + k, nz)}, device_id_type=MESH
         )
-        greeted += 1
+    greeted = nz + 1 + above_first + at_last
 
     lane = lax.broadcasted_iota(jnp.int32, (ROWS, lanes), 1)
     lane_group = lane >> 2
@@ -90,7 +111,7 @@
         return right, left
 
     inner = pl.ds(8, xs)
-    halos = [
+    z_copies = [
         pltpu.make_async_remote_copy(
             field.at[zs - 2 : zs], cells.at[0:2, inner, :], z_send.at[0], z_recv.at[0],
             device_id={"gz": right_z}, device_id_type=MESH,
@@ -99,23 +120,33 @@
             field.at[0:2], cells.at[zs + 2 : zs + 4, inner, :], z_send.at[1], z_recv.at[1],
             device_id={"gz": left_z}, device_id_type=MESH,
         ),
-        pltpu.make_async_remote_copy(
-            field.at[:, xs - 2 : xs, :], cells.at[2 : zs + 2, 6:8, :], x_send.at[0], x_recv.at[0],
-            device_id={"gx": right_x}, device_id_type=MESH,
-        ),
-        pltpu.make_async_remote_copy(
-            field.at[:, 0:2, :], cells.at[2 : zs + 2, xs + 8 : xs + 10, :], x_send.at[1],
-            x_recv.at[1], device_id={"gx": left_x}, device_id_type=MESH,
-        ),
     ]
+    x_right = pltpu.make_async_remote_copy(
+        field.at[:, xs - 2 : xs, :], cells.at[2 : zs + 2, 6:8, :], x_send.at[0], x_recv.at[0],
+        device_id={"gx": right_x}, device_id_type=MESH,
+    )
+    x_left = pltpu.make_async_remote_copy(
+        field.at[:, 0:2, :], cells.at[2 : zs + 2, xs + 8 : xs + 10, :], x_send.at[1],
+        x_recv.at[1], device_id={"gx": left_x}, device_id_type=MESH,
+    )
 
     load(0).wait()
     pack(0)
     pl.semaphore_wait(barrier, greeted)
-    for copy in halos:
+    for copy in z_copies:
         copy.start()
     for copy in y_copies(0):
         copy.start()
+
+    @pl.when(mx > 0)
+    def _():
+        pl.semaphore_signal(entered.at[1], inc=1, device_id={"gx": left_x}, device_id_type=MESH)
+        x_left.start()
+
+    @pl.when(mx == nx - 1)
+    def _():
+        pl.semaphore_signal(entered.at[0], inc=1, device_id={"gx": right_x}, device_id_type=MESH)
+        x_right.start()
 
     @pl.loop(1, blocks)
     def _(step):
@@ -209,18 +240,36 @@
             device_id={"gz": block_of(step)}, device_id_type=MESH,
         )
 
-    for copy in halos:
+    for copy in z_copies:
         copy.wait_recv()
     for z in (0, 1, zs + 2, zs + 3):
         eighth[z, inner, :] = 0.125 * cells[z, inner, :]
 
-    @pl.loop(0, zs // 8)
-    def _(i):
-        for rows in (pl.ds(6, 2), pl.ds(xs + 8, 2)):
-            eighth[pl.ds(i * 8 + 2, 8), rows, :] = 0.125 * cells[pl.ds(i * 8 + 2, 8), rows, :]
-
     @pl.loop(0, blocks)
     def _(step):
+        @pl.when(step == SEND_X)
+        def _():
+            @pl.when(mx == 0)
+            def _():
+                pl.semaphore_wait(entered.at[0], 1)
+                x_left.start()
+
+            @pl.when(mx < nx - 1)
+            def _():
+                pl.semaphore_wait(entered.at[1], 1)
+                x_right.start()
+
+        @pl.when(step == blocks - 3)
+        def _():
+            x_left.wait_recv()
+            x_right.wait_recv()
+
+            @pl.loop(0, zs // 8)
+            def _(i):
+                for rows in (pl.ds(6, 2), pl.ds(xs + 8, 2)):
+                    z8 = pl.ds(i * 8 + 2, 8)
+                    eighth[z8, rows, :] = 0.125 * cells[z8, rows, :]
+
         for copy in y_copies(step):
             copy.wait_recv()
         correction(step)
@@ -257,7 +306,7 @@
         out[c] = image[c]
     out[3] = 1.0 - jnp.exp2(optical)
 
-    for copy in halos:
+    for copy in (x_left, x_right, *z_copies):
         copy.wait_send()
     for step in range(blocks):
         for copy in y_copies(step):
@@ -288,6 +337,7 @@
             pltpu.VMEM((nz, 4, ROWS, lanes), f32),
             dma((blocks,)), dma((2,)), dma((2,)), dma((2,)), dma((2,)),
             dma((2, blocks)), dma((2, blocks)), dma((blocks,)), dma((nz,)),
+            pltpu.SemaphoreType.REGULAR((2,)),
         ],
         compiler_params=pltpu.CompilerParams(collective_id=0, has_side_effects=True),
     )(field, peaks, tint, light)

time: 37.3 us -> 32.6 us (0.87)
  the two profiles are of different devices: /device:TPU:1 before, /device:TPU:32 now
where the time goes in v1:
time: 32.6 us; the launch traced here: 32.4 us
  Pallas kernels  31 us (95%)
  local copies, waits for them, and re-layouts  1.38 us (4%)
    pallas_call x1, Pallas kernels, render(): pl.pallas_call(functools.partial(kernel, nx, ny, nz, zs * nz), out_shape=...  31 us
    unnamed x1, local copies, waits for them, and re-layouts  1.38 us

profile of v1, /device:TPU:32, one launch (start us, length us, event | category | flops | bytes accessed | tf_op | source)
XLA Modules:
  0.0 32.4 jit_solution(6812679929540168559)
XLA Ops:
  0.0 31.0 %shard_map.46 = f32[4,16,128]{2,1,0:T(8,128)} custom-call(f32[128,128,128]{2,1,0:T(8,128)} %field.1, f32[4]{0:T(128)} %peaks.1, f32[3]{0:T(128)} %tint.1, f32[3]{0:T(128)} %light.1), custom_call_target="tpu_custom_call" | custom-call | tf_op jit(solution)/shard_map/pallas_call | solution.py:326
  31.1 1.4 %copy.6 = f32[4,16,128]{2,1,0:T(8,128)} copy(f32[4,16,128]{2,1,0:T(8,128)} %shard_map.46) | data formatting | bytes 65536

commit v2 on v1

--- a/solution.py
+++ b/solution.py
@@ -13,13 +13,12 @@
 MESH = pl.DeviceIdType.MESH
 ROWS = 16
 GROUP = 32
-UNROLL = 32
-SEND_X = 1
+SEND_X = 0
 
 
 def kernel(
     nx, ny, nz, depth, field, peaks, tint, light, out,
-    cells, eighth, border, to_right, to_left, from_left, from_right, piece, pieces,
+    cells, eighth, pair, pair_eighth, thick, border, to_right, to_left, from_left, from_right, piece, pieces,
     load_sem, x_send, x_recv, z_send, z_recv, y_send, y_recv, p_send, p_recv, entered,
 ):
     zs, xs, lanes = field.shape
@@ -30,20 +29,21 @@
     left_y, right_y = lax.rem(my + ny - 1, ny), lax.rem(my + 1, ny)
     left_z, right_z = lax.rem(mz + nz - 1, nz), lax.rem(mz + 1, nz)
 
-    bordering = 1 - (lax.rem(mz, nz - 1) + nz - 2) // (nz - 1)
-    parity = lax.rem(mz, 2)
+    above_zero, is_last = (mz + nz - 1) // nz, (mz + 1) // nz
+    zero_step = max(1, nz - 4)
+
+    def reached(step, bound):
+        return (step + nz - bound) // nz
 
     def block_of(step):
-        from_0, from_1, from_2 = ((step + k) // nz for k in (3, 2, 1))
-        inside = lax.rem(mz + step, nz - 2) + 1
-        border_one = bordering * inside + (1 - bordering) * parity * (nz - 1)
-        border_two = bordering * (nz - 1 - mz) + (1 - bordering) * (1 - parity) * (nz - 1)
-        return (
-            (1 - from_0) * inside
-            + (from_0 - from_1) * border_one
-            + (from_1 - from_2) * border_two
-            + from_2 * mz
-        )
+        at_own = reached(step, nz - 1)
+        at_zero = reached(step, zero_step) - reached(step, zero_step + 1)
+        at_late = reached(step, nz - 2) - at_own
+        place = step + 1 - above_zero * reached(step, zero_step + 1)
+        inner_block = place + above_zero * reached(place, mz)
+        late = is_last * inner_block + (1 - is_last) * (nz - 1)
+        other = at_late * late + (1 - at_late) * inner_block
+        return (1 - at_own) * (1 - at_zero * above_zero) * other + at_own * mz
 
     def rows_of(step):
         return pl.multiple_of(block_of(step) * ROWS, ROWS)
@@ -81,6 +81,21 @@
     lane_group = lane >> 2
     lane_column = lane & 3
     first_pair = lane_column < 2
+
+    unit = extinction / depth * LOG2E
+    first = peaks[0]
+    slopes = [4.0 * LOG2E * (peaks[i] - first) for i in range(1, peaks.shape[0])]
+    offsets = [
+        math.log2(unit) - 2.0 * LOG2E * (peaks[i] * peaks[i] - first * first)
+        for i in range(1, peaks.shape[0])
+    ]
+
+    def thickness(f):
+        bumps = unit
+        for k in range(len(slopes)):
+            bumps = bumps + jnp.exp2(f * slopes[k] + offsets[k])
+        away = f - first
+        return jnp.exp2(away * away * (-2.0 * LOG2E)) * bumps
 
     def pack(step):
         rows = rows_of(step)
@@ -91,6 +106,10 @@
             for g in range(groups):
                 v = cells[2 + g * GROUP + z, pl.ds(rows + 8, ROWS), :]
                 eighth[2 + g * GROUP + z, pl.ds(rows + 8, ROWS), :] = 0.125 * v
+                thick[g * GROUP + z, pl.ds(rows, ROWS), :] = thickness(v)
+                two = v - pltpu.roll(v, 2, 1)
+                pair[g * GROUP + z, pl.ds(rows, ROWS), :] = two
+                pair_eighth[g * GROUP + z, pl.ds(rows, ROWS), :] = 0.125 * two
                 packed[g] = jnp.where(here, pltpu.roll(v, (4 * z + 2) % lanes, 1), packed[g])
         for g in range(groups):
             border[g, pl.ds(rows, ROWS), :] = packed[g]
@@ -130,56 +149,59 @@
         x_recv.at[1], device_id={"gx": left_x}, device_id_type=MESH,
     )
 
-    load(0).wait()
-    pack(0)
-    pl.semaphore_wait(barrier, greeted)
-    for copy in z_copies:
-        copy.start()
-    for copy in y_copies(0):
-        copy.start()
-
-    @pl.when(mx > 0)
-    def _():
-        pl.semaphore_signal(entered.at[1], inc=1, device_id={"gx": left_x}, device_id_type=MESH)
-        x_left.start()
-
-    @pl.when(mx == nx - 1)
-    def _():
-        pl.semaphore_signal(entered.at[0], inc=1, device_id={"gx": right_x}, device_id_type=MESH)
-        x_right.start()
-
-    @pl.loop(1, blocks)
+    greet = (nz - 1 - mz) // 2 + 1
+
+    @pl.loop(0, blocks)
     def _(step):
         load(step).wait()
         pack(step)
-        for copy in y_copies(step):
-            copy.start()
-
-    def correction(step):
+
+        @pl.when(step == greet)
+        def _():
+            pl.semaphore_wait(barrier, greeted)
+            for copy in z_copies:
+                copy.start()
+
+            @pl.loop(0, greet)
+            def _(ready):
+                for copy in y_copies(ready):
+                    copy.start()
+
+            @pl.when(mx > 0)
+            def _():
+                pl.semaphore_signal(
+                    entered.at[1], inc=1, device_id={"gx": left_x}, device_id_type=MESH
+                )
+                x_left.start()
+
+            @pl.when(mx == nx - 1)
+            def _():
+                pl.semaphore_signal(
+                    entered.at[0], inc=1, device_id={"gx": right_x}, device_id_type=MESH
+                )
+                x_right.start()
+
+        @pl.when(step >= greet)
+        def _():
+            for copy in y_copies(step):
+                copy.start()
+
+    def corrections(step, p):
         rows = rows_of(step)
-        for g in range(0, groups, 2):
-            left, right = from_left[step, g // 2], from_right[step, g // 2]
-            for odd in range(2):
-                if odd:
-                    outer = jnp.where(
-                        first_pair, pltpu.roll(left, lanes - 2, 1), pltpu.roll(right, 2, 1)
-                    )
-                else:
-                    outer = jnp.where(first_pair, left, right)
-                diff = outer - border[g + odd, pl.ds(rows, ROWS), :]
-                p2, p1 = pltpu.roll(diff, lanes - 2, 1), pltpu.roll(diff, lanes - 1, 1)
-                m2, m1 = pltpu.roll(diff, 2, 1), pltpu.roll(diff, 1, 1)
-                far = 0.125 * jnp.where(first_pair, -p2, m2)
-                near = jnp.where(lane_column == 1, p1, jnp.where(lane_column == 2, -m1, 0.0))
-                border[g + odd, pl.ds(rows, ROWS), :] = near + far
-
-    unit = extinction / depth * LOG2E
-    first = peaks[0]
-    slopes = [4.0 * LOG2E * (peaks[i] - first) for i in range(1, peaks.shape[0])]
-    offsets = [
-        math.log2(unit) - 2.0 * LOG2E * (peaks[i] * peaks[i] - first * first)
-        for i in range(1, peaks.shape[0])
-    ]
+        left, right = from_left[step, p], from_right[step, p]
+        fixes = []
+        for odd in range(2):
+            if odd:
+                left, right = pltpu.roll(left, lanes - 2, 1), pltpu.roll(right, 2, 1)
+            outer = jnp.where(first_pair, left, right)
+            diff = outer - border[2 * p + odd, pl.ds(rows, ROWS), :]
+            p2, p1 = pltpu.roll(diff, lanes - 2, 1), pltpu.roll(diff, lanes - 1, 1)
+            m2, m1 = pltpu.roll(diff, 2, 1), pltpu.roll(diff, 1, 1)
+            far = 0.125 * jnp.where(first_pair, -p2, m2)
+            near = jnp.where(lane_column == 1, p1, jnp.where(lane_column == 2, -m1, 0.0))
+            fixes.append(near + far)
+        return fixes
+
     tints = [0.5 * tint[c] for c in range(3)]
     lights = [0.7 * light[c] for c in range(3)]
     edge = (lane < 2) | (lane >= lanes - 2)
@@ -189,33 +211,29 @@
         base = rows + 8
         mid = pl.ds(base, ROWS)
 
-        def one_group(g, carry):
-            fix_all = border[g, pl.ds(rows, ROWS), :]
-
-            def some(i, carry):
+        def one_pair(p, carry):
+            fixes = corrections(step, p)
+
+            def one_group(odd, carry):
                 total, trans, s0, s1, s2, s3 = carry
-                for j in range(UNROLL):
-                    zl = i * UNROLL + j
-                    z = g * GROUP + zl + 2
-                    f, f8 = cells[z, mid, :], eighth[z, mid, :]
+                for zl in range(GROUP):
+                    z = (2 * p + odd) * GROUP + zl + 2
+                    f = cells[z, mid, :]
                     gz = (cells[z + 1, mid, :] - cells[z - 1, mid, :]) - (
                         eighth[z + 2, mid, :] - eighth[z - 2, mid, :]
                     )
                     gx = (
                         cells[z, pl.ds(base + 1, ROWS), :] - cells[z, pl.ds(base - 1, ROWS), :]
                     ) - (eighth[z, pl.ds(base + 2, ROWS), :] - eighth[z, pl.ds(base - 2, ROWS), :])
-                    gy = (pltpu.roll(f, lanes - 1, 1) - pltpu.roll(f, 1, 1)) - (
-                        pltpu.roll(f8, lanes - 2, 1) - pltpu.roll(f8, 2, 1)
+                    two8 = pair_eighth[z - 2, pl.ds(rows, ROWS), :]
+                    gy = pltpu.roll(pair[z - 2, pl.ds(rows, ROWS), :], lanes - 1, 1) - (
+                        pltpu.roll(two8, lanes - 2, 1) + two8
                     )
-                    fix = pltpu.roll(fix_all, (2 * lanes - 2 - 4 * zl) % lanes, 1)
+                    fix = pltpu.roll(fixes[odd], (2 * lanes - 2 - 4 * zl) % lanes, 1)
                     gy = jnp.where(edge, gy + fix, gy)
                     inverse = lax.rsqrt((gx * gx + gy * gy) + (gz * gz + 2.25))
                     lit = jnp.abs(gx * lights[0] + gy * lights[1] + gz * lights[2])
-                    bumps = unit
-                    for k in range(len(slopes)):
-                        bumps = bumps + jnp.exp2(f * slopes[k] + offsets[k])
-                    away = f - first
-                    total = total - jnp.exp2(away * away * (-2.0 * LOG2E)) * bumps
+                    total = total - thick[z - 2, pl.ds(rows, ROWS), :]
                     after = jnp.exp2(total)
                     shaded = (trans - after) * (0.3 + lit * inverse)
                     trans = after
@@ -225,13 +243,11 @@
                     s3 = s3 + shaded * jnp.tanh(f * tints[2])
                 return total, trans, s0, s1, s2, s3
 
-            if UNROLL == GROUP:
-                return some(0, carry)
-            return lax.fori_loop(0, GROUP // UNROLL, some, carry)
+            return one_group(1, one_group(0, carry))
 
         zero = jnp.zeros((ROWS, lanes), jnp.float32)
         start = (zero, zero + 1.0, zero, zero, zero, zero)
-        total, _, s0, s1, s2, s3 = lax.fori_loop(0, groups, one_group, start)
+        total, _, s0, s1, s2, s3 = lax.fori_loop(0, groups // 2, one_pair, start)
         return 0.5 * (s0 + s1), 0.5 * (s0 + s2), 0.5 * (s0 + s3), total
 
     def p_copy(step):
@@ -259,7 +275,7 @@
                 pl.semaphore_wait(entered.at[1], 1)
                 x_right.start()
 
-        @pl.when(step == blocks - 3)
+        @pl.when(step == zero_step)
         def _():
             x_left.wait_recv()
             x_right.wait_recv()
@@ -272,7 +288,6 @@
 
         for copy in y_copies(step):
             copy.wait_recv()
-        correction(step)
         results = march(step)
 
         @pl.when(step < blocks - 1)
@@ -331,6 +346,9 @@
         scratch_shapes=[
             pltpu.VMEM((zs + 4, xs + 16, lanes), f32),
             pltpu.VMEM((zs + 4, xs + 16, lanes), f32),
+            pltpu.VMEM((zs, xs, lanes), f32),
+            pltpu.VMEM((zs, xs, lanes), f32),
+            pltpu.VMEM((zs, xs, lanes), f32),
             pltpu.VMEM((groups, xs, lanes), f32),
             packed, packed, packed, packed,
             pltpu.VMEM((blocks, 4, ROWS, lanes), f32),
@@ -339,7 +357,9 @@
             dma((2, blocks)), dma((2, blocks)), dma((blocks,)), dma((nz,)),
             pltpu.SemaphoreType.REGULAR((2,)),
         ],
-        compiler_params=pltpu.CompilerParams(collective_id=0, has_side_effects=True),
+        compiler_params=pltpu.CompilerParams(
+            collective_id=0, has_side_effects=True, vmem_limit_bytes=62 << 20
+        ),
     )(field, peaks, tint, light)
 
 

time: 32.6 us -> 29.8 us (0.914)
  the two profiles are of different devices: /device:TPU:32 before, /device:TPU:1 now
where the time goes in v2:
time: 29.8 us; the launch traced here: 29.4 us
  Pallas kernels  28 us (94%)
  local copies, waits for them, and re-layouts  1.38 us (5%)
    pallas_call x1, Pallas kernels, render(): pl.pallas_call(functools.partial(kernel, nx, ny, nz, zs * nz), out_shape=...  28 us
    unnamed x1, local copies, waits for them, and re-layouts  1.38 us

profile of v2, /device:TPU:1, one launch (start us, length us, event | category | flops | bytes accessed | tf_op | source)
XLA Modules:
  0.0 29.4 jit_solution(11036801772024834528)
XLA Ops:
  0.0 28.0 %shard_map.46 = f32[4,16,128]{2,1,0:T(8,128)} custom-call(f32[128,128,128]{2,1,0:T(8,128)} %field.1, f32[4]{0:T(128)} %peaks.1, f32[3]{0:T(128)} %tint.1, f32[3]{0:T(128)} %light.1), custom_call_target="tpu_custom_call" | custom-call | tf_op jit(solution)/shard_map/pallas_call | solution.py:341
  28.0 1.4 %copy.6 = f32[4,16,128]{2,1,0:T(8,128)} copy(f32[4,16,128]{2,1,0:T(8,128)} %shard_map.46) | data formatting | bytes 65536

commit v3 on v2

--- a/solution.py
+++ b/solution.py
@@ -13,13 +13,14 @@
 MESH = pl.DeviceIdType.MESH
 ROWS = 16
 GROUP = 32
-SEND_X = 0
+AHEAD = 3
+SEND_X = 2
 
 
 def kernel(
-    nx, ny, nz, depth, field, peaks, tint, light, out,
-    cells, eighth, pair, pair_eighth, thick, border, to_right, to_left, from_left, from_right, piece, pieces,
-    load_sem, x_send, x_recv, z_send, z_recv, y_send, y_recv, p_send, p_recv, entered,
+    nx, ny, nz, depth, field, peaks_in, tint_in, light_in, pieces, peaks, tint, light,
+    cells, eighth, pair, pair_eighth, thick, border, to_right, to_left, from_left, from_right, piece,
+    scalar_sem, load_sem, x_send, x_recv, z_send, z_recv, y_send, y_recv, p_send, p_recv, entered,
 ):
     zs, xs, lanes = field.shape
     groups = zs // GROUP
@@ -30,20 +31,27 @@
     left_z, right_z = lax.rem(mz + nz - 1, nz), lax.rem(mz + 1, nz)
 
     above_zero, is_last = (mz + nz - 1) // nz, (mz + 1) // nz
-    zero_step = max(1, nz - 4)
+    zero_step = nz - 3
 
     def reached(step, bound):
         return (step + nz - bound) // nz
 
+    early = above_zero * (1 - reached(mz, nz // 2))
+
     def block_of(step):
         at_own = reached(step, nz - 1)
-        at_zero = reached(step, zero_step) - reached(step, zero_step + 1)
-        at_late = reached(step, nz - 2) - at_own
+        at_first = reached(step, zero_step) - reached(step, zero_step + 1)
+        at_second = reached(step, nz - 2) - at_own
         place = step + 1 - above_zero * reached(step, zero_step + 1)
         inner_block = place + above_zero * reached(place, mz)
-        late = is_last * inner_block + (1 - is_last) * (nz - 1)
-        other = at_late * late + (1 - at_late) * inner_block
-        return (1 - at_own) * (1 - at_zero * above_zero) * other + at_own * mz
+        first_block = above_zero * early * (nz - 1) + (1 - above_zero) * inner_block
+        second_block = (1 - early) * (is_last * inner_block + (1 - is_last) * (nz - 1))
+        return (
+            at_own * mz
+            + at_first * first_block
+            + at_second * second_block
+            + (1 - at_own - at_first - at_second) * inner_block
+        )
 
     def rows_of(step):
         return pl.multiple_of(block_of(step) * ROWS, ROWS)
@@ -55,8 +63,16 @@
             load_sem.at[step],
         )
 
-    for step in range(blocks):
+    for step in range(AHEAD):
         load(step).start()
+    scalars = [
+        pltpu.make_async_copy(source, target, scalar_sem.at[k])
+        for k, (source, target) in enumerate(
+            ((peaks_in, peaks), (tint_in, tint), (light_in, light))
+        )
+    ]
+    for copy in scalars:
+        copy.start()
 
     barrier = pltpu.get_barrier_semaphore()
     above_first, at_last = (mx + nx - 1) // nx, (mx + 1) // nx
@@ -77,6 +93,8 @@
         )
     greeted = nz + 1 + above_first + at_last
 
+    for copy in scalars:
+        copy.wait()
     lane = lax.broadcasted_iota(jnp.int32, (ROWS, lanes), 1)
     lane_group = lane >> 2
     lane_column = lane & 3
@@ -154,6 +172,11 @@
     @pl.loop(0, blocks)
     def _(step):
         load(step).wait()
+
+        @pl.when(step + AHEAD < blocks)
+        def _():
+            load(step + AHEAD).start()
+
         pack(step)
 
         @pl.when(step == greet)
@@ -290,36 +313,22 @@
             copy.wait_recv()
         results = march(step)
 
+        for c in range(4):
+            piece[step, c] = results[c]
+
         @pl.when(step < blocks - 1)
         def _():
-            for c in range(4):
-                piece[step, c] = results[c]
             p_copy(step).start()
 
-        @pl.when(step == blocks - 1)
-        def _():
-            for c in range(4):
-                pieces[mz, c] = results[c]
-
+    own = pltpu.make_async_copy(piece.at[blocks - 1], pieces.at[mz], p_recv.at[mz])
+    own.start()
     for k in range(1, nz):
         source = lax.rem(mz + k, nz)
         pltpu.make_async_remote_copy(
             piece.at[0], pieces.at[source], p_send.at[0], p_recv.at[source],
             device_id={"gz": source}, device_id_type=MESH,
         ).wait_recv()
-
-    before = None
-    for k in range(nz):
-        if k == 0:
-            image = [pieces[0, c] for c in range(3)]
-            optical = pieces[0, 3]
-        else:
-            before = jnp.exp2(optical)
-            image = [image[c] + before * pieces[k, c] for c in range(3)]
-            optical = optical + pieces[k, 3]
-    for c in range(3):
-        out[c] = image[c]
-    out[3] = 1.0 - jnp.exp2(optical)
+    own.wait()
 
     for copy in (x_left, x_right, *z_copies):
         copy.wait_send()
@@ -330,6 +339,18 @@
         p_copy(step).wait_send()
 
 
+def composite(nz, pieces, out):
+    image = [pieces[0, c] for c in range(3)]
+    optical = pieces[0, 3]
+    for k in range(1, nz):
+        before = jnp.exp2(optical)
+        image = [image[c] + before * pieces[k, c] for c in range(3)]
+        optical = optical + pieces[k, 3]
+    for c in range(3):
+        out[c] = image[c]
+    out[3] = 1.0 - jnp.exp2(optical)
+
+
 def render(sizes, field, peaks, tint, light):
     nx, ny, nz = sizes
     zs, xs, lanes = field.shape
@@ -337,13 +358,13 @@
     f32 = jnp.float32
     packed = pltpu.VMEM((blocks, groups // 2, ROWS, lanes), f32)
     dma = pltpu.SemaphoreType.DMA
-    smem = pl.BlockSpec(memory_space=pltpu.SMEM)
-    return pl.pallas_call(
+    pieces = pl.pallas_call(
         functools.partial(kernel, nx, ny, nz, zs * nz),
-        out_shape=jax.ShapeDtypeStruct((4, ROWS, lanes), f32),
-        in_specs=[pl.BlockSpec(memory_space=pl.ANY), smem, smem, smem],
-        out_specs=pl.BlockSpec(memory_space=pltpu.VMEM),
+        out_shape=jax.ShapeDtypeStruct((nz, 4, ROWS, lanes), f32),
+        in_specs=[pl.BlockSpec(memory_space=pl.ANY)] * 4,
+        out_specs=pl.BlockSpec(memory_space=pl.ANY),
         scratch_shapes=[
+            *(pltpu.SMEM(a.shape, f32) for a in (peaks, tint, light)),
             pltpu.VMEM((zs + 4, xs + 16, lanes), f32),
             pltpu.VMEM((zs + 4, xs + 16, lanes), f32),
             pltpu.VMEM((zs, xs, lanes), f32),
@@ -352,8 +373,7 @@
             pltpu.VMEM((groups, xs, lanes), f32),
             packed, packed, packed, packed,
             pltpu.VMEM((blocks, 4, ROWS, lanes), f32),
-            pltpu.VMEM((nz, 4, ROWS, lanes), f32),
-            dma((blocks,)), dma((2,)), dma((2,)), dma((2,)), dma((2,)),
+            dma((3,)), dma((blocks,)), dma((2,)), dma((2,)), dma((2,)), dma((2,)),
             dma((2, blocks)), dma((2, blocks)), dma((blocks,)), dma((nz,)),
             pltpu.SemaphoreType.REGULAR((2,)),
         ],
@@ -361,6 +381,10 @@
             collective_id=0, has_side_effects=True, vmem_limit_bytes=62 << 20
         ),
     )(field, peaks, tint, light)
+    return pl.pallas_call(
+        functools.partial(composite, nz),
+        out_shape=jax.ShapeDtypeStruct((4, ROWS, lanes), f32),
+    )(pieces)
 
 
 def solution(mesh):

time: 29.8 us -> 27.7 us (0.930)
  local copies, waits for them, and re-layouts: 1.38 us -> 0 us
  Pallas kernels: 28 us -> 27.6 us
    pallas_call x1, Pallas kernels: 28 us -> 26 us  [render(): pl.pallas_call(functools.partial(kernel, nx, ny, nz, zs * nz), out_shape=...]
    pallas_call x0 -> x1, Pallas kernels: none -> 1.59 us  [render(): pl.pallas_call(functools.partial(composite, nz), out_shape=jax.ShapeDtype...]
    unnamed x1 -> x0, local copies, waits for them, and re-layouts: 1.38 us -> none
where the time goes in v3:
time: 27.7 us; the launch traced here: 27.6 us
  Pallas kernels  27.6 us (100%)
    pallas_call x1, Pallas kernels, render(): pl.pallas_call(functools.partial(kernel, nx, ny, nz, zs * nz), out_shape=...  26 us
    pallas_call x1, Pallas kernels, render(): pl.pallas_call(functools.partial(composite, nz), out_shape=jax.ShapeDtype...  1.59 us

profile of v3, /device:TPU:1, one launch (start us, length us, event | category | flops | bytes accessed | tf_op | source)
XLA Modules:
  0.0 27.6 jit_solution(3905378344548049506)
XLA Ops:
  0.0 26.0 %shard_map.46.pieces = f32[8,4,16,128]{3,2,1,0:T(8,128)} custom-call(f32[128,128,128]{2,1,0:T(8,128)} %field.1, f32[4]{0:T(128)} %peaks_in.1, f32[3]{0:T(128)} %tint_in.1, f32[3]{0:T(128)} %light_in.1), custom_call_target="tpu_custom_call" | custom-call | tf_op jit(solution)/shard_map/pallas_call | solution.py:361
  26.0 1.6 %shard_map.47 = f32[4,16,128]{2,1,0:T(8,128)} custom-call(f32[8,4,16,128]{3,2,1,0:T(8,128)} %shard_map.46.pieces), custom_call_target="tpu_custom_call" | custom-call | tf_op jit(solution)/shard_map/pallas_call | solution.py:384

commit v4 on v3

--- a/solution.py
+++ b/solution.py
@@ -147,17 +147,31 @@
         )
         return right, left
 
-    inner = pl.ds(8, xs)
-    z_copies = [
-        pltpu.make_async_remote_copy(
-            field.at[zs - 2 : zs], cells.at[0:2, inner, :], z_send.at[0], z_recv.at[0],
-            device_id={"gz": right_z}, device_id_type=MESH,
-        ),
-        pltpu.make_async_remote_copy(
-            field.at[0:2], cells.at[zs + 2 : zs + 4, inner, :], z_send.at[1], z_recv.at[1],
-            device_id={"gz": left_z}, device_id_type=MESH,
-        ),
-    ]
+    half = xs // 2
+    z_copies = []
+    for part in range(2):
+        rows = pl.ds(part * half, half)
+        inner_rows = pl.ds(8 + part * half, half)
+        z_copies.append((
+            pltpu.make_async_remote_copy(
+                field.at[zs - 2 : zs, rows, :], cells.at[0:2, inner_rows, :],
+                z_send.at[0, part], z_recv.at[0, part],
+                device_id={"gz": right_z}, device_id_type=MESH,
+            ),
+            pltpu.make_async_remote_copy(
+                field.at[0:2, rows, :], cells.at[zs + 2 : zs + 4, inner_rows, :],
+                z_send.at[1, part], z_recv.at[1, part],
+                device_id={"gz": left_z}, device_id_type=MESH,
+            ),
+        ))
+
+    def z_arrived(part):
+        inner_rows = pl.ds(8 + part * half, half)
+        for copy in z_copies[part]:
+            copy.wait_recv()
+        for z in (0, 1, zs + 2, zs + 3):
+            eighth[z, inner_rows, :] = 0.125 * cells[z, inner_rows, :]
+
     x_right = pltpu.make_async_remote_copy(
         field.at[:, xs - 2 : xs, :], cells.at[2 : zs + 2, 6:8, :], x_send.at[0], x_recv.at[0],
         device_id={"gx": right_x}, device_id_type=MESH,
@@ -167,7 +181,7 @@
         x_recv.at[1], device_id={"gx": left_x}, device_id_type=MESH,
     )
 
-    greet = (nz - 1 - mz) // 2 + 1
+    greet = 4 - 2 * reached(mz, 2) - reached(mz, nz - 2)
 
     @pl.loop(0, blocks)
     def _(step):
@@ -182,7 +196,7 @@
         @pl.when(step == greet)
         def _():
             pl.semaphore_wait(barrier, greeted)
-            for copy in z_copies:
+            for copy in (*z_copies[0], *z_copies[1]):
                 copy.start()
 
             @pl.loop(0, greet)
@@ -279,13 +293,14 @@
             device_id={"gz": block_of(step)}, device_id_type=MESH,
         )
 
-    for copy in z_copies:
-        copy.wait_recv()
-    for z in (0, 1, zs + 2, zs + 3):
-        eighth[z, inner, :] = 0.125 * cells[z, inner, :]
+    z_arrived(0)
 
     @pl.loop(0, blocks)
     def _(step):
+        @pl.when(step == 2)
+        def _():
+            z_arrived(1)
+
         @pl.when(step == SEND_X)
         def _():
             @pl.when(mx == 0)
@@ -330,7 +345,7 @@
         ).wait_recv()
     own.wait()
 
-    for copy in (x_left, x_right, *z_copies):
+    for copy in (x_left, x_right, *z_copies[0], *z_copies[1]):
         copy.wait_send()
     for step in range(blocks):
         for copy in y_copies(step):
@@ -373,7 +388,7 @@
             pltpu.VMEM((groups, xs, lanes), f32),
             packed, packed, packed, packed,
             pltpu.VMEM((blocks, 4, ROWS, lanes), f32),
-            dma((3,)), dma((blocks,)), dma((2,)), dma((2,)), dma((2,)), dma((2,)),
+            dma((3,)), dma((blocks,)), dma((2,)), dma((2,)), dma((2, 2)), dma((2, 2)),
             dma((2, blocks)), dma((2, blocks)), dma((blocks,)), dma((nz,)),
             pltpu.SemaphoreType.REGULAR((2,)),
         ],

time: 27.7 us -> 27.2 us (0.982)
  Pallas kernels: 27.6 us -> 27 us
    pallas_call x1, Pallas kernels: 26 us -> 25.4 us  [render(): pl.pallas_call(functools.partial(kernel, nx, ny, nz, zs * nz), out_shape=...]
where the time goes in v4:
time: 27.2 us; the launch traced here: 27 us
  Pallas kernels  27 us (99%)
    pallas_call x1, Pallas kernels, render(): pl.pallas_call(functools.partial(kernel, nx, ny, nz, zs * nz), out_shape=...  25.4 us
    pallas_call x1, Pallas kernels, render(): pl.pallas_call(functools.partial(composite, nz), out_shape=jax.ShapeDtype...  1.59 us

profile of v4, /device:TPU:1, one launch (start us, length us, event | category | flops | bytes accessed | tf_op | source)
XLA Modules:
  0.0 27.0 jit_solution(357580916951061349)
XLA Ops:
  0.0 25.4 %shard_map.46.pieces = f32[8,4,16,128]{3,2,1,0:T(8,128)} custom-call(f32[128,128,128]{2,1,0:T(8,128)} %field.1, f32[4]{0:T(128)} %peaks_in.1, f32[3]{0:T(128)} %tint_in.1, f32[3]{0:T(128)} %light_in.1), custom_call_target="tpu_custom_call" | custom-call | tf_op jit(solution)/shard_map/pallas_call | solution.py:376
  25.4 1.6 %shard_map.47 = f32[4,16,128]{2,1,0:T(8,128)} custom-call(f32[8,4,16,128]{3,2,1,0:T(8,128)} %shard_map.46.pieces), custom_call_target="tpu_custom_call" | custom-call | tf_op jit(solution)/shard_map/pallas_call | solution.py:399

commit v5 on v4

--- a/solution.py
+++ b/solution.py
@@ -118,7 +118,6 @@
     def pack(step):
         rows = rows_of(step)
 
-        packed = [jnp.zeros((ROWS, lanes), jnp.float32)] * groups
         for z in range(GROUP):
             here = lane_group == z
             for g in range(groups):
@@ -128,11 +127,13 @@
                 two = v - pltpu.roll(v, 2, 1)
                 pair[g * GROUP + z, pl.ds(rows, ROWS), :] = two
                 pair_eighth[g * GROUP + z, pl.ds(rows, ROWS), :] = 0.125 * two
-                packed[g] = jnp.where(here, pltpu.roll(v, (4 * z + 2) % lanes, 1), packed[g])
-        for g in range(groups):
-            border[g, pl.ds(rows, ROWS), :] = packed[g]
+                pltpu.store(
+                    border.at[g, pl.ds(rows, ROWS), :],
+                    pltpu.roll(v, (4 * z + 2) % lanes, 1),
+                    mask=here,
+                )
         for g in range(0, groups, 2):
-            even, odd = packed[g], packed[g + 1]
+            even, odd = border[g, pl.ds(rows, ROWS), :], border[g + 1, pl.ds(rows, ROWS), :]
             to_right[step, g // 2] = jnp.where(first_pair, even, pltpu.roll(odd, 2, 1))
             to_left[step, g // 2] = jnp.where(first_pair, pltpu.roll(odd, lanes - 2, 1), even)
 
@@ -181,7 +182,7 @@
         x_recv.at[1], device_id={"gx": left_x}, device_id_type=MESH,
     )
 
-    greet = 4 - 2 * reached(mz, 2) - reached(mz, nz - 2)
+    greet = 4 - 2 * reached(mz, 2) - reached(mz, nz - 2) - is_last
 
     @pl.loop(0, blocks)
     def _(step):

time: 27.2 us -> 27.1 us (level)
  no operation moved by 1% of the time
where the time goes in v5:
time: 27.1 us; the launch traced here: 26.8 us
  Pallas kernels  26.8 us (99%)
    pallas_call x1, Pallas kernels, render(): pl.pallas_call(functools.partial(kernel, nx, ny, nz, zs * nz), out_shape=...  25.2 us
    pallas_call x1, Pallas kernels, render(): pl.pallas_call(functools.partial(composite, nz), out_shape=jax.ShapeDtype...  1.59 us

profile of v5, /device:TPU:1, one launch (start us, length us, event | category | flops | bytes accessed | tf_op | source)
XLA Modules:
  0.0 26.8 jit_solution(12062171380498047845)
XLA Ops:
  0.0 25.2 %shard_map.46.pieces = f32[8,4,16,128]{3,2,1,0:T(8,128)} custom-call(f32[128,128,128]{2,1,0:T(8,128)} %field.1, f32[4]{0:T(128)} %peaks_in.1, f32[3]{0:T(128)} %tint_in.1, f32[3]{0:T(128)} %light_in.1), custom_call_target="tpu_custom_call" | custom-call | tf_op jit(solution)/shard_map/pallas_call | solution.py:377
  25.2 1.6 %shard_map.47 = f32[4,16,128]{2,1,0:T(8,128)} custom-call(f32[8,4,16,128]{3,2,1,0:T(8,128)} %shard_map.46.pieces), custom_call_target="tpu_custom_call" | custom-call | tf_op jit(solution)/shard_map/pallas_call | solution.py:400
